TPU v7x, 512 devices: a whole 4x8x8 slice. The times are simulated.
512 devices in a mesh: req: 32 (over z_hi, x, core), seq: 16 (over z_lo, y).
Axes of the slice: x: 4, y: 8, z: 8 (z_hi: 4, z_lo: 2; z = z_hi * 2 + z_lo), core: 2. Of those that a mesh axis runs over, the one named last changes fastest.
Arguments:
- layer_input: bfloat16 [32, 256, 2048], P('req', 'seq'), may hold values from -3 to 3
- queries: bfloat16 [32, 256, 4096], P('req', 'seq'), may hold values from -4.5 to 4.5
- fresh_kv: bfloat16 [32, 256, 1024], P('req', 'seq'), may hold values from -4.5 to 4.5
- cache_kv: bfloat16 [32, 1792, 1024], P('req', 'seq'), may hold values from -4.5 to 4.5
- cached_len: int32 [32], P('req'), may hold values from 2 to 1792, as said below
- out_weight: bfloat16 [4096, 2048], P('seq', 'req'), may hold values from -0.09375 to 0.09375
- norm_gain: float32 [2048], replicated, may hold values from 0.5 to 1.5
- routes: int32 [32, 256, 8], P('req', 'seq'), may hold values from 0 to 127, all different within a row; in each aligned block of 16 rows (0 to 15, 16 to 31, ..., all dimensions but the last counted through in order) at most 2 rows name the same one
- route_gates: float32 [32, 256, 8], P('req', 'seq'), may hold values from 0.2 to 1
- w_gate_up: bfloat16 [512, 2048, 384], P(('req', 'seq')), may hold values from -0.125 to 0.125
- w_down: bfloat16 [512, 192, 2048], P(('req', 'seq')), may hold values from -0.21875 to 0.21875
Outputs:
- output: bfloat16 [32, 256, 2048], P('req', 'seq')
Inputs may be any that keep to these rules, and one draw needn't show every extreme that they name: Request r has cached_len[r] valid cached rows; some request has exactly 1792. `routes`: each token names 8 different experts; among the 16 tokens of one device (aligned blocks), no expert is named more than 2 times.
All inputs are finite; a program needn't handle non-finite values.
Results may differ from a plain program's by a relative error of at most 0.03.
Values may be sent and summed in bfloat16 or wider, within the bound.
A program may use at most 64 MiB of HBM per device.

v0:
```python
import math
import jax
import jax.numpy as jnp
from jax import lax
from jax.sharding import PartitionSpec as P

QH = 32
KVH = 4
HD = 128
EXPERTS = 128
TOP = 8
CAP = 2
neg_large = -1e30
epsilon = 1e-06


def local(
    layer_input,
    queries,
    fresh_kv,
    cache_kv,
    cached_len,
    out_weight,
    norm_gain,
    routes,
    route_gates,
    w_gate_up,
    w_down,
):
    new_dev = queries.shape[1]
    cache_dev = cache_kv.shape[1]
    query_width = queries.shape[2]
    kv_width = fresh_kv.shape[2] // 2
    seq_count = lax.axis_size("seq")
    req_count = lax.axis_size("req")
    group_size = QH // KVH
    scale = 1.0 / math.sqrt(HD)
    block_rows = cache_dev + new_dev
    length = cached_len[0]
    query_pos = lax.axis_index("seq") * new_dev + jnp.arange(new_dev, dtype=jnp.int32)
    grouped = queries[0].reshape(new_dev, KVH, group_size, HD)
    key_block = jnp.concatenate([cache_kv[0], fresh_kv[0]], 0)
    shard_rows = lax.all_gather(key_block, "seq", axis=0, tiled=True)
    row_count = shard_rows.shape[0]
    row_index = jnp.arange(row_count, dtype=jnp.int32)
    source_dev = row_index // block_rows
    within = row_index % block_rows
    in_cache = within < cache_dev
    cache_live = source_dev * cache_dev + within < length
    fresh_live = (source_dev * new_dev + within - cache_dev)[None, :] <= query_pos[:, None]
    visible = jnp.where(in_cache[None, :], cache_live[None, :], fresh_live)
    running_max = jnp.full((new_dev, KVH, group_size), neg_large, jnp.float32)
    key_part = shard_rows[:, :kv_width].reshape(row_count, KVH, HD)
    value_part = shard_rows[:, kv_width:].reshape(row_count, KVH, HD)
    scores = (
        jnp.einsum("ngqc,pgc->ngqp", grouped, key_part, preferred_element_type=jnp.float32) * scale
    )
    mask = visible[:, None, None, :]
    scores = jnp.where(mask, scores, neg_large)
    new_max = jnp.maximum(running_max, jnp.max(scores, axis=-1))
    weights = jnp.where(mask, jnp.exp(scores - new_max[..., None]), 0.0)
    denominator = jnp.sum(weights, axis=-1)
    mixed_values = jnp.einsum(
        "ngqp,pgc->ngqc",
        weights.astype(jnp.bfloat16),
        value_part,
        preferred_element_type=jnp.float32,
    )
    numerator = mixed_values
    running_max, denominator, numerator = (new_max, denominator, numerator)
    attended = (
        (numerator / denominator[..., None]).reshape(new_dev, query_width).astype(jnp.bfloat16)
    )
    by_heads = lax.all_to_all(attended, "seq", split_axis=1, concat_axis=0, tiled=True)
    proj_full = lax.all_gather(out_weight, "req", axis=1, tiled=True)
    projected = lax.psum_scatter(
        jnp.dot(by_heads, proj_full, preferred_element_type=jnp.float32).astype(jnp.bfloat16),
        "seq",
        scatter_dimension=0,
        tiled=True,
    ).astype(jnp.float32)
    residual = (layer_input[0].astype(jnp.float32) + projected).astype(jnp.bfloat16)
    residual_f = residual.astype(jnp.float32)
    normed = (
        residual_f
        * lax.rsqrt(jnp.mean(residual_f * residual_f, axis=-1, keepdims=True) + epsilon)
        * norm_gain
    ).astype(jnp.bfloat16)
    owned_count = EXPERTS // req_count
    slab_count = w_gate_up.shape[0]
    split_count = seq_count * slab_count // owned_count
    hidden_part = w_down.shape[1]
    model_width = normed.shape[1]
    pair_count = new_dev * TOP
    chosen = routes[0].reshape(pair_count)
    onehot = (chosen[:, None] == jnp.arange(EXPERTS, dtype=jnp.int32)[None, :]).astype(jnp.int32)
    earlier = jnp.cumsum(onehot, axis=0) - onehot
    slot_at = jnp.sum(earlier * onehot, axis=1)
    target = chosen * CAP + slot_at
    placed = (target[:, None] == jnp.arange(EXPERTS * CAP, dtype=jnp.int32)[None, :]).astype(
        jnp.float32
    )
    placed_rows = placed.reshape(new_dev, TOP, EXPERTS * CAP)
    picker = jnp.sum(placed_rows, axis=1).astype(jnp.bfloat16)
    outgoing = lax.dot_general(
        picker, normed, (((0,), (0,)), ((), ())), preferred_element_type=jnp.float32
    )
    outgoing = outgoing.astype(jnp.bfloat16).reshape(req_count, owned_count, CAP, model_width)
    combine_rows = jnp.sum(placed_rows * route_gates[0][:, :, None], axis=1)
    arrived_req = lax.all_to_all(outgoing, "req", split_axis=0, concat_axis=0, tiled=True)
    spread_out = jnp.broadcast_to(
        arrived_req[:, :, None], (req_count, owned_count, split_count, CAP, model_width)
    )
    arrived = lax.all_to_all(
        spread_out.reshape(req_count, seq_count, slab_count, CAP, model_width),
        "seq",
        split_axis=1,
        concat_axis=1,
        tiled=True,
    )
    token_rows = arrived[:, :, 0].reshape(req_count * seq_count * CAP, model_width)
    both = jnp.dot(token_rows, w_gate_up[0], preferred_element_type=jnp.float32)
    hidden = (jax.nn.silu(both[:, :hidden_part]) * both[:, hidden_part:]).astype(jnp.bfloat16)
    part_out = jnp.dot(hidden, w_down[0], preferred_element_type=jnp.float32).astype(jnp.bfloat16)
    produced_list = [part_out.reshape(req_count, seq_count, CAP, model_width)]
    produced = jnp.stack(produced_list, axis=2)
    returned = lax.all_to_all(produced, "seq", split_axis=1, concat_axis=1, tiled=True)
    grouped_parts = returned.reshape(req_count, owned_count, split_count, CAP, model_width).astype(
        jnp.float32
    )
    result = lax.all_to_all(
        jnp.sum(grouped_parts, axis=2).astype(jnp.bfloat16),
        "req",
        split_axis=0,
        concat_axis=0,
        tiled=True,
    )
    expert_rows = result.reshape(EXPERTS * CAP, model_width).astype(jnp.float32)
    mixture = jnp.dot(combine_rows, expert_rows, precision=lax.Precision.HIGHEST)
    output = (residual_f + mixture).astype(jnp.bfloat16)
    return output[None]


def solution(mesh):
    return jax.shard_map(
        local,
        mesh=mesh,
        in_specs=(
            P("req", "seq", None),
            P("req", "seq", None),
            P("req", "seq", None),
            P("req", "seq", None),
            P("req"),
            P("seq", "req"),
            P(),
            P("req", "seq", None),
            P("req", "seq", None),
            P(("req", "seq"), None, None),
            P(("req", "seq"), None, None),
        ),
        out_specs=P("req", "seq", None),
        check_vma=False,
    )
```

profile of v0, /device:TPU:12, one launch (start us, length us, event | category | flops | bytes accessed | tf_op | source)
XLA Modules:
  0.0 570.8 jit_solution(9128146810409177649)
XLA Ops:
  6.5 1.2 copy.99
  12.1 91.9 %all-gather.3.cloned.1.call-done = bf16[2048,1024]{0,1:T(8,128)(2,1)} async-done(((bf16[128,1024]{0,1:T(8,128)(2,1)}), bf16[2048,1024]{0,1:T(8,128)(2,1)}) %all-gather.3.cloned.1.call-update) | async-done | bytes 4194320 | tf_op jit(solution)/shard_map/all_gather | solution.py:43
  103.9 2.8 fusion.51
  107.7 1.2 fusion.1
  110.8 7.8 %all-to-all-start = ((bf16[16,16,256]{2,0,1:T(8,128)(2,1)}), bf16[16,16,256]{2,0,1:T(8,128)(2,1)S(1)}, u32[]{:S(2)}, u32[]{:S(2)}) async-start(bf16[16,16,256]{2,0,1:T(8,128)(2,1)} %copy.105), calls=%async_computation | async-start | bytes 262144 | tf_op jit(solution)/shard_map/all_to_all | solution.py:74
  118.7 46.1 %all-gather.5.cloned.1.call-done = bf16[256,2048]{0,1:T(8,128)(2,1)} async-done(((bf16[256,64]{0,1:T(8,128)(2,1)}), bf16[256,2048]{0,1:T(8,128)(2,1)}) %all-gather.5.cloned.1.call-update) | async-done | bytes 1048592 | tf_op jit(solution)/shard_map/all_gather | solution.py:75
  164.8 2.7 convolution_convert_fusion.1
  168.6 69.4 %reduce-scatter.2.cloned.1.call-done = bf16[16,2048]{1,0:T(8,128)(2,1)} async-done(((bf16[256,2048]{1,0:T(8,128)(2,1)}), bf16[16,2048]{1,0:T(8,128)(2,1)}) %reduce-scatter.2.cloned.1.call-update) | async-done | bytes 65552 | tf_op jit(solution)/shard_map/reduce_scatter | solution.py:76
  239.0 1.3 convolution_convert_fusion.2
  240.3 1.5 reshape.147
  241.9 38.3 %all_to_all.36 = bf16[32,4,2,2048]{3,2,1,0:T(2,128)(2,1)S(1)} all-to-all(bf16[32,4,2,2048]{3,2,1,0:T(2,128)(2,1)} %reshape.147), channel_id=1, replica_groups=mesh['req'=32,'seq'=16] {'req'}, dimensions={0} | all-to-all | bytes 2097152 | tf_op jit(solution)/shard_map/all_to_all | solution.py:110
  281.0 5.4 broadcast_in_dim.64
  286.4 98.3 %all_to_all.37 = bf16[32,16,1,2,2048]{4,3,0,2,1:T(2,128)(2,1)S(1)} all-to-all(bf16[32,16,1,2,2048]{4,3,0,2,1:T(2,128)(2,1)} %bitcast.81), channel_id=1, replica_groups=mesh['req'=32,'seq'=16] {'seq'}, dimensions={1} | all-to-all | bytes 8388608 | tf_op jit(solution)/shard_map/all_to_all | solution.py:114
  384.8 6.5 %copy.111 = bf16[32,16,1,2,2048]{4,3,1,0,2:T(2,128)(2,1)} copy(bf16[32,16,1,2,2048]{4,3,0,2,1:T(2,128)(2,1)S(1)} %all_to_all.37) | data formatting | bytes 8388608 | tf_op jit(solution)/shard_map/all_to_all | solution.py:114
  391.2 7.2 %reshape_squeeze.8 = bf16[1024,2048]{1,0:T(8,128)(2,1)} reshape(bf16[32,16,1,2,2048]{4,3,1,0,2:T(2,128)(2,1)} %copy.111) | data formatting | bytes 8388608 | tf_op jit(solution)/shard_map/reshape;squeeze | solution.py:121
  398.4 4.1 fusion.8
  402.5 3.2 convolution_convert_fusion
  405.8 7.6 %stack_reshape.3 = bf16[32,16,1,2,2048]{4,3,1,0,2:T(2,128)(2,1)} reshape(bf16[1024,2048]{1,0:T(8,128)(2,1)} %convolution_convert_fusion) | data formatting | bytes 8388608 | tf_op jit(solution)/shard_map/stack;reshape | solution.py:126
  413.4 6.0 %copy.112 = bf16[32,16,1,2,2048]{4,3,0,2,1:T(2,128)(2,1)S(1)} copy(bf16[32,16,1,2,2048]{4,3,1,0,2:T(2,128)(2,1)} %stack_reshape.3) | data formatting | bytes 8388608 | tf_op jit(solution)/shard_map/stack;reshape | solution.py:126
  419.5 97.5 %all_to_all.38 = bf16[32,16,1,2,2048]{4,3,0,2,1:T(2,128)(2,1)} all-to-all(bf16[32,16,1,2,2048]{4,3,0,2,1:T(2,128)(2,1)S(1)} %copy.112), channel_id=1, replica_groups=mesh['req'=32,'seq'=16] {'seq'}, dimensions={1} | all-to-all | bytes 8388608 | tf_op jit(solution)/shard_map/all_to_all | solution.py:127
  516.9 7.2 %bitcast_reduce_fusion = bf16[32,4,2,2048]{3,2,0,1:T(2,128)(2,1)S(1)} fusion(bf16[32,4,4,2,2048]{4,3,0,2,1:T(2,128)(2,1)} %bitcast.82), kind=kLoop, calls=%fused_computation | loop fusion | flops 1572864 | bytes 5242880 | tf_op jit(solution)/shard_map/reduce_sum | solution.py:132
  525.3 36.3 %all_to_all.39 = bf16[32,4,2,2048]{3,2,1,0:T(2,128)(2,1)} all-to-all(bf16[32,4,2,2048]{3,2,1,0:T(2,128)(2,1)S(1)} %copy.113), channel_id=1, replica_groups=mesh['req'=32,'seq'=16] {'req'}, dimensions={0} | all-to-all | bytes 2097152 | tf_op jit(solution)/shard_map/all_to_all | solution.py:131
  561.6 1.5 reshape.150
  563.1 1.2 fusion.4
  (49 shorter events, 10.5 us)
Async XLA Ops:
  6.5 391.9 %copy-start = (bf16[1,2048,384]{2,1,0:T(8,128)(2,1)S(1)}, bf16[1,2048,384]{2,1,0:T(8,128)(2,1)}, u32[]{:S(2)}) copy-start(bf16[1,2048,384]{2,1,0:T(8,128)(2,1)} %param.20) | copy-start | bytes 4718596
  6.5 97.4 %all-gather.3.cloned.1.call-start = ((), (), s32[]{:S(2)}) async-start(), calls=%async_computation.6 | async-start | bytes 4456448 | tf_op jit(solution)/shard_map/all_gather | solution.py:43
  9.6 155.2 %all-gather.5.cloned.1.call-start = ((), (), s32[]{:S(2)}) async-start(), calls=%async_computation.7 | async-start | bytes 1081344 | tf_op jit(solution)/shard_map/all_gather | solution.py:75
  110.0 57.5 %copy-start.3 = (s32[1,16,8]{1,2,0:T(8,128)S(1)}, s32[1,16,8]{1,2,0:T(8,128)}, u32[]{:S(2)}) copy-start(s32[1,16,8]{1,2,0:T(8,128)} %param.18) | copy-start | bytes 1540
  110.0 58.4 %copy-start.5 = (f32[1,16,8]{1,2,0:T(8,128)S(1)}, f32[1,16,8]{1,2,0:T(8,128)}, u32[]{:S(2)}) copy-start(f32[1,16,8]{1,2,0:T(8,128)} %param.19) | copy-start | bytes 1540
  110.0 128.0 %copy-start.1 = (bf16[1,16,2048]{2,1,0:T(8,128)(2,1)S(1)}, bf16[1,16,2048]{2,1,0:T(8,128)(2,1)}, u32[]{:S(2)}) copy-start(bf16[1,16,2048]{2,1,0:T(8,128)(2,1)} %param.11) | copy-start | bytes 196612
  110.0 129.0 %copy-start.4 = (f32[2048]{0:T(1024)S(1)}, f32[2048]{0:T(1024)}, u32[]{:S(2)}) copy-start(f32[2048]{0:T(1024)} %param.17) | copy-start | bytes 24580
  110.8 54.0 %all-to-all-start = ((bf16[16,16,256]{2,0,1:T(8,128)(2,1)}), bf16[16,16,256]{2,0,1:T(8,128)(2,1)S(1)}, u32[]{:S(2)}, u32[]{:S(2)}) async-start(bf16[16,16,256]{2,0,1:T(8,128)(2,1)} %copy.105), calls=%async_computation | async-start | bytes 262144 | tf_op jit(solution)/shard_map/all_to_all | solution.py:74
  118.6 119.4 %reduce-scatter.2.cloned.1.call-start = ((), (), s32[]{:S(2)}) async-start(), calls=%async_computation.8 | async-start | bytes 1114112 | tf_op jit(solution)/shard_map/reduce_scatter | solution.py:76
  398.4 4.1 copy-start.6
  524.2 39.0 %copy-start.2 = (bf16[16,2048]{1,0:T(8,128)(2,1)S(1)}, bf16[16,2048]{1,0:T(8,128)(2,1)}, u32[]{:S(2)}) copy-start(bf16[16,2048]{1,0:T(8,128)(2,1)} %reduce-scatter.2.cloned.1.call-done) | copy-start | bytes 196612
Sparse Core Ops, SparseCore 0:
  9.7 94.1 all-gather.2
  107.1 57.6 all-gather.4
  167.6 70.3 reduce-scatter.1
where the time goes:
time: 572 us; the launch traced here: 571 us
  blocking collectives  271 us (47%)
  waiting for transfers between devices  208 us (36%)
  local copies, waits for them, and re-layouts  44.8 us (8%)
  matrix products  14.5 us (3%)
  between operations  14 us (2%)
  other arithmetic  10.9 us (2%)
  starting transfers between devices  7.91 us (1%)
    all_to_all x1, blocking collectives, local(): lax.all_to_all(spread_out.reshape(req_count, seq_count, slab_count, CAP,...  98.3 us
    all_to_all x1, blocking collectives, local(): lax.all_to_all(produced, 'seq', split_axis=1, concat_axis=1, tiled=True)  97.5 us
    all_gather x1, waiting for transfers between devices, local(): shard_rows = lax.all_gather(key_block, 'seq', axis=0, tiled=True)  91.9 us
    reduce_scatter x1, waiting for transfers between devices, local(): lax.psum_scatter(jnp.dot(by_heads, proj_full, preferred_element_type=jnp....  69.4 us
    all_gather x1, waiting for transfers between devices, local(): proj_full = lax.all_gather(out_weight, 'req', axis=1, tiled=True)  46.1 us
    all_to_all x1, blocking collectives, local(): lax.all_to_all(outgoing, 'req', split_axis=0, concat_axis=0, tiled=True)  38.3 us
    all_to_all x1, blocking collectives, local(): lax.all_to_all(jnp.sum(grouped_parts, axis=2).astype(jnp.bfloat16), 'req'...  36.3 us
    another operation x2, local copies, waits for them, and re-layouts, local(): produced = jnp.stack(produced_list, axis=2)  13.7 us
  transfers between devices with their start and end apart: 4, of which 3 were waited for; matrix products, arithmetic and copies ran while one was open for 2% of the time, Pallas kernels for 0%

commit v1 on v0

--- a/solution.py
+++ b/solution.py
@@ -40,7 +40,12 @@
     query_pos = lax.axis_index("seq") * new_dev + jnp.arange(new_dev, dtype=jnp.int32)
     grouped = queries[0].reshape(new_dev, KVH, group_size, HD)
     key_block = jnp.concatenate([cache_kv[0], fresh_kv[0]], 0)
-    shard_rows = lax.all_gather(key_block, "seq", axis=0, tiled=True)
+    kept_rows = []
+    for _ in range(lax.axis_size("seq")):
+        kept_rows.append(key_block)
+    taken_in = jnp.stack(kept_rows, axis=0)
+    prior = lax.all_to_all(taken_in, "seq", 0, 0)
+    shard_rows = jnp.concatenate(prior, axis=0)
     row_count = shard_rows.shape[0]
     row_index = jnp.arange(row_count, dtype=jnp.int32)
     source_dev = row_index // block_rows

time: 572 us -> 548 us (0.958)
  waiting for transfers between devices: 208 us -> 173 us
  starting transfers between devices: 7.91 us -> 17.6 us
    all_to_all x0 -> x1, waiting for transfers between devices: none -> 94.4 us  [local(): prior = lax.all_to_all(taken_in, 'seq', 0, 0)]
    all_gather x1 -> x0, waiting for transfers between devices: 91.9 us -> none  [local(): shard_rows = lax.all_gather(key_block, 'seq', axis=0, tiled=True)]
    all_gather x1, waiting for transfers between devices: 46.1 us -> 0.02 us  [local(): proj_full = lax.all_gather(out_weight, 'req', axis=1, tiled=True)]
    all_to_all x0 -> x1, starting transfers between devices: none -> 9.5 us  [local(): prior = lax.all_to_all(taken_in, 'seq', 0, 0)]
    all_to_all x1, waiting for transfers between devices: 0.01 us -> 7.84 us  [local(): lax.all_to_all(attended, 'seq', split_axis=1, concat_axis=0, tiled=True)]
where the time goes in v1:
time: 548 us; the launch traced here: 547 us
  blocking collectives  271 us (49%)
  waiting for transfers between devices  173 us (32%)
  local copies, waits for them, and re-layouts  45.1 us (8%)
  starting transfers between devices  17.6 us (3%)
  matrix products  14.6 us (3%)
  between operations  14.3 us (3%)
  other arithmetic  11.2 us (2%)
    all_to_all x1, blocking collectives, local(): lax.all_to_all(spread_out.reshape(req_count, seq_count, slab_count, CAP,...  98.5 us
    all_to_all x1, blocking collectives, local(): lax.all_to_all(produced, 'seq', split_axis=1, concat_axis=1, tiled=True)  97.5 us
    all_to_all x1, waiting for transfers between devices, local(): prior = lax.all_to_all(taken_in, 'seq', 0, 0)  94.4 us
    reduce_scatter x1, waiting for transfers between devices, local(): lax.psum_scatter(jnp.dot(by_heads, proj_full, preferred_element_type=jnp....  70.4 us
    all_to_all x1, blocking collectives, local(): lax.all_to_all(outgoing, 'req', split_axis=0, concat_axis=0, tiled=True)  38.2 us
    all_to_all x1, blocking collectives, local(): lax.all_to_all(jnp.sum(grouped_parts, axis=2).astype(jnp.bfloat16), 'req'...  36.4 us
    another operation x2, local copies, waits for them, and re-layouts, local(): produced = jnp.stack(produced_list, axis=2)  13.7 us
  transfers between devices with their start and end apart: 4, of which 3 were waited for; matrix products, arithmetic and copies ran while one was open for 2% of the time, Pallas kernels for 0%

profile of v1, /device:TPU:12, one launch (start us, length us, event | category | flops | bytes accessed | tf_op | source)
XLA Modules:
  0.0 546.7 jit_solution(10823000766652491730)
XLA Ops:
  7.8 2.8 stack.2
  10.6 9.5 %all-to-all-start = ((bf16[16,128,1024]{1,2,0:T(8,128)(2,1)}), bf16[16,128,1024]{1,2,0:T(8,128)(2,1)}, u32[]{:S(2)}, u32[]{:S(2)}) async-start(bf16[16,128,1024]{1,2,0:T(8,128)(2,1)} %stack.2), calls=%async_computation | async-start | bytes 8388608 | tf_op jit(solution)/shard_map/all_to_all | solution.py:47
  21.7 94.4 %all-to-all-done = bf16[16,128,1024]{1,2,0:T(8,128)(2,1)} async-done(((bf16[16,128,1024]{1,2,0:T(8,128)(2,1)}), bf16[16,128,1024]{1,2,0:T(8,128)(2,1)}, u32[]{:S(2)}, u32[]{:S(2)}) %all-to-all-start) | async-done | bytes 4194336 | tf_op jit(solution)/shard_map/all_to_all | solution.py:47
  116.1 2.8 copy_bitcast_fusion
  120.3 1.2 fusion.1
  123.4 8.1 %all-to-all-start.1 = ((bf16[16,16,256]{2,0,1:T(8,128)(2,1)}), bf16[16,16,256]{2,0,1:T(8,128)(2,1)S(1)}, u32[]{:S(2)}, u32[]{:S(2)}) async-start(bf16[16,16,256]{2,0,1:T(8,128)(2,1)} %copy.104), calls=%async_computation.1 | async-start | bytes 262144 | tf_op jit(solution)/shard_map/all_to_all | solution.py:79
  131.5 7.8 %all-to-all-done.1 = bf16[16,16,256]{2,0,1:T(8,128)(2,1)S(1)} async-done(((bf16[16,16,256]{2,0,1:T(8,128)(2,1)}), bf16[16,16,256]{2,0,1:T(8,128)(2,1)S(1)}, u32[]{:S(2)}, u32[]{:S(2)}) %all-to-all-start.1) | async-done | bytes 131104 | tf_op jit(solution)/shard_map/all_to_all | solution.py:79
  139.4 2.7 convolution_convert_fusion.1
  143.2 70.4 %reduce-scatter.2.cloned.1.call-done = bf16[16,2048]{1,0:T(8,128)(2,1)} async-done(((bf16[256,2048]{1,0:T(8,128)(2,1)}), bf16[16,2048]{1,0:T(8,128)(2,1)}) %reduce-scatter.2.cloned.1.call-update) | async-done | bytes 65552 | tf_op jit(solution)/shard_map/reduce_scatter | solution.py:81
  214.6 1.3 convolution_convert_fusion.2
  215.9 1.5 reshape.153
  217.4 38.2 %all_to_all.41 = bf16[32,4,2,2048]{3,2,1,0:T(2,128)(2,1)S(1)} all-to-all(bf16[32,4,2,2048]{3,2,1,0:T(2,128)(2,1)} %reshape.153), channel_id=1, replica_groups=mesh['req'=32,'seq'=16] {'req'}, dimensions={0} | all-to-all | bytes 2097152 | tf_op jit(solution)/shard_map/all_to_all | solution.py:115
  256.4 5.4 broadcast_in_dim.64
  261.8 98.5 %all_to_all.42 = bf16[32,16,1,2,2048]{4,3,0,2,1:T(2,128)(2,1)S(1)} all-to-all(bf16[32,16,1,2,2048]{4,3,0,2,1:T(2,128)(2,1)} %bitcast.86), channel_id=1, replica_groups=mesh['req'=32,'seq'=16] {'seq'}, dimensions={1} | all-to-all | bytes 8388608 | tf_op jit(solution)/shard_map/all_to_all | solution.py:119
  360.3 6.5 %copy.110 = bf16[32,16,1,2,2048]{4,3,1,0,2:T(2,128)(2,1)} copy(bf16[32,16,1,2,2048]{4,3,0,2,1:T(2,128)(2,1)S(1)} %all_to_all.42) | data formatting | bytes 8388608 | tf_op jit(solution)/shard_map/all_to_all | solution.py:119
  366.8 7.2 %reshape_squeeze.8 = bf16[1024,2048]{1,0:T(8,128)(2,1)} reshape(bf16[32,16,1,2,2048]{4,3,1,0,2:T(2,128)(2,1)} %copy.110) | data formatting | bytes 8388608 | tf_op jit(solution)/shard_map/reshape;squeeze | solution.py:126
  374.0 4.1 fusion.8
  378.1 3.2 convolution_convert_fusion
  381.3 7.6 %stack_reshape.3 = bf16[32,16,1,2,2048]{4,3,1,0,2:T(2,128)(2,1)} reshape(bf16[1024,2048]{1,0:T(8,128)(2,1)} %convolution_convert_fusion) | data formatting | bytes 8388608 | tf_op jit(solution)/shard_map/stack;reshape | solution.py:131
  389.0 6.0 %copy.111 = bf16[32,16,1,2,2048]{4,3,0,2,1:T(2,128)(2,1)S(1)} copy(bf16[32,16,1,2,2048]{4,3,1,0,2:T(2,128)(2,1)} %stack_reshape.3) | data formatting | bytes 8388608 | tf_op jit(solution)/shard_map/stack;reshape | solution.py:131
  395.0 97.5 %all_to_all.43 = bf16[32,16,1,2,2048]{4,3,0,2,1:T(2,128)(2,1)} all-to-all(bf16[32,16,1,2,2048]{4,3,0,2,1:T(2,128)(2,1)S(1)} %copy.111), channel_id=1, replica_groups=mesh['req'=32,'seq'=16] {'seq'}, dimensions={1} | all-to-all | bytes 8388608 | tf_op jit(solution)/shard_map/all_to_all | solution.py:132
  492.5 7.2 %bitcast_reduce_fusion = bf16[32,4,2,2048]{3,2,0,1:T(2,128)(2,1)S(1)} fusion(bf16[32,4,4,2,2048]{4,3,0,2,1:T(2,128)(2,1)} %bitcast.87), kind=kLoop, calls=%fused_computation.1 | loop fusion | flops 1572864 | bytes 5242880 | tf_op jit(solution)/shard_map/reduce_sum | solution.py:137
  500.8 36.4 %all_to_all.44 = bf16[32,4,2,2048]{3,2,1,0:T(2,128)(2,1)} all-to-all(bf16[32,4,2,2048]{3,2,1,0:T(2,128)(2,1)S(1)} %copy.112), channel_id=1, replica_groups=mesh['req'=32,'seq'=16] {'req'}, dimensions={0} | all-to-all | bytes 2097152 | tf_op jit(solution)/shard_map/all_to_all | solution.py:136
  537.2 1.5 reshape.156
  (51 shorter events, 10.6 us)
Async XLA Ops:
  6.5 367.4 %copy-start = (bf16[1,2048,384]{2,1,0:T(8,128)(2,1)S(1)}, bf16[1,2048,384]{2,1,0:T(8,128)(2,1)}, u32[]{:S(2)}) copy-start(bf16[1,2048,384]{2,1,0:T(8,128)(2,1)} %param.20) | copy-start | bytes 4718596
  10.6 10.9 %copy-start.3 = (bf16[1,16,4096]{2,1,0:T(8,128)(2,1)S(1)}, bf16[1,16,4096]{2,1,0:T(8,128)(2,1)}, u32[]{:S(2)}) copy-start(bf16[1,16,4096]{2,1,0:T(8,128)(2,1)} %param.12) | copy-start | bytes 393220
  10.6 105.5 %all-to-all-start = ((bf16[16,128,1024]{1,2,0:T(8,128)(2,1)}), bf16[16,128,1024]{1,2,0:T(8,128)(2,1)}, u32[]{:S(2)}, u32[]{:S(2)}) async-start(bf16[16,128,1024]{1,2,0:T(8,128)(2,1)} %stack.2), calls=%async_computation | async-start | bytes 8388608 | tf_op jit(solution)/shard_map/all_to_all | solution.py:47
  20.1 111.4 %all-gather.2.cloned.1.call-start = ((), (), s32[]{:S(2)}) async-start(), calls=%async_computation.7 | async-start | bytes 1081344 | tf_op jit(solution)/shard_map/all_gather | solution.py:80
  122.6 19.5 %copy-start.4 = (s32[1,16,8]{1,2,0:T(8,128)S(1)}, s32[1,16,8]{1,2,0:T(8,128)}, u32[]{:S(2)}) copy-start(s32[1,16,8]{1,2,0:T(8,128)} %param.18) | copy-start | bytes 1540
  122.6 20.4 %copy-start.6 = (f32[1,16,8]{1,2,0:T(8,128)S(1)}, f32[1,16,8]{1,2,0:T(8,128)}, u32[]{:S(2)}) copy-start(f32[1,16,8]{1,2,0:T(8,128)} %param.19) | copy-start | bytes 1540
  122.6 91.0 %copy-start.1 = (bf16[1,16,2048]{2,1,0:T(8,128)(2,1)S(1)}, bf16[1,16,2048]{2,1,0:T(8,128)(2,1)}, u32[]{:S(2)}) copy-start(bf16[1,16,2048]{2,1,0:T(8,128)(2,1)} %param.11) | copy-start | bytes 196612
  122.6 92.0 %copy-start.5 = (f32[2048]{0:T(1024)S(1)}, f32[2048]{0:T(1024)}, u32[]{:S(2)}) copy-start(f32[2048]{0:T(1024)} %param.17) | copy-start | bytes 24580
  123.4 16.0 %all-to-all-start.1 = ((bf16[16,16,256]{2,0,1:T(8,128)(2,1)}), bf16[16,16,256]{2,0,1:T(8,128)(2,1)S(1)}, u32[]{:S(2)}, u32[]{:S(2)}) async-start(bf16[16,16,256]{2,0,1:T(8,128)(2,1)} %copy.104), calls=%async_computation.1 | async-start | bytes 262144 | tf_op jit(solution)/shard_map/all_to_all | solution.py:79
  131.5 82.1 %reduce-scatter.2.cloned.1.call-start = ((), (), s32[]{:S(2)}) async-start(), calls=%async_computation.8 | async-start | bytes 1114112 | tf_op jit(solution)/shard_map/reduce_scatter | solution.py:81
  374.0 4.1 copy-start.7
  499.7 39.0 %copy-start.2 = (bf16[16,2048]{1,0:T(8,128)(2,1)S(1)}, bf16[16,2048]{1,0:T(8,128)(2,1)}, u32[]{:S(2)}) copy-start(bf16[16,2048]{1,0:T(8,128)(2,1)} %reduce-scatter.2.cloned.1.call-done) | copy-start | bytes 196612
Sparse Core Ops, SparseCore 0:
  24.1 78.9 all-gather.1
  142.2 71.3 reduce-scatter.1
